TPU v7x, 32 devices: a whole 2x2x4 slice. The times are simulated.
32 devices in a mesh: sec: 16 (over z, y, x), tile: 2 (over core).
Axes of the slice: x: 2, y: 2, z: 4, core: 2. Of those that a mesh axis runs over, the one named last changes fastest.
Arguments:
- probe: float32 [2, 16, 512], P(None, 'tile'), may hold values from -5 to 5
- offsets: int32 [4], replicated, may hold values from 0 to 511
- phase: float32 [32, 16, 512], P('sec', 'tile'), may hold values from -1.5 to 1.5
- absorption: float32 [32, 16, 512], P('sec', 'tile'), may hold values from 0 to 0.02
- measured: float32 [4, 16, 512], P(None, 'tile'), may hold values from 0.2 to 2
Outputs:
- gradient: float32 [32, 2, 16, 512], P('sec', None, 'tile')
All inputs are finite; a program needn't handle non-finite values.
Results may differ from a plain program's by a relative error of at most 0.00013.
Values sent between devices are 32-bit elements; how exact they have to be, the bound alone decides.
A program may use at most 64 MiB of HBM per device.

v0:
```python
import jax
import jax.numpy as jnp
from jax import lax
from jax.sharding import PartitionSpec as P

PROP_RE = 0.004
PROP_IM = 0.0314


def padded(value, sides, width):
    for axis, dim in sides:
        size, length = (lax.axis_size(axis), value.shape[dim])
        up = [(i, (i + 1) % size) for i in range(size - 1)]
        down = [(j, i) for i, j in up]
        last = lax.slice_in_dim(value, length - width, length, axis=dim)
        initial = lax.slice_in_dim(value, 0, width, axis=dim)
        before = lax.ppermute(last, axis, up)
        after = lax.ppermute(initial, axis, down)
        value = jnp.concatenate([before, value, after], axis=dim)
    return value


def passed_along(value, axis, steps):
    count = lax.axis_size(axis)
    initial, last = (max(0, -steps), min(count, count - steps))
    return lax.ppermute(value, axis, [(source, source + steps) for source in range(initial, last)])


def complex_product(multiplier, operand):
    real_part = (
        multiplier[..., 0, :, :] * operand[..., 0, :, :]
        - multiplier[..., 1, :, :] * operand[..., 1, :, :]
    )
    imag_part = (
        multiplier[..., 0, :, :] * operand[..., 1, :, :]
        + multiplier[..., 1, :, :] * operand[..., 0, :, :]
    )
    return jnp.stack([real_part, imag_part], -3)


def conjugate_product(multiplier, operand):
    real_part = (
        multiplier[..., 0, :, :] * operand[..., 0, :, :]
        + multiplier[..., 1, :, :] * operand[..., 1, :, :]
    )
    imag_part = (
        multiplier[..., 0, :, :] * operand[..., 1, :, :]
        - multiplier[..., 1, :, :] * operand[..., 0, :, :]
    )
    return jnp.stack([real_part, imag_part], -3)


def propagate(extended, coupling):
    centre = extended[..., 1:-1, :]
    laplacian = (
        extended[..., :-2, :]
        + extended[..., 2:, :]
        + jnp.roll(centre, 1, -1)
        + jnp.roll(centre, -1, -1)
        - 4.0 * centre
    )
    real_part = (
        centre[..., 0, :, :]
        + PROP_RE * laplacian[..., 0, :, :]
        - coupling * laplacian[..., 1, :, :]
    )
    imag_part = (
        centre[..., 1, :, :]
        + PROP_RE * laplacian[..., 1, :, :]
        + coupling * laplacian[..., 0, :, :]
    )
    return jnp.stack([real_part, imag_part], -3)


def forward_section(wavefield, transmission):
    slice_count = transmission.shape[0]
    inputs = []
    for layer_index in range(slice_count):
        inputs.append(wavefield)
        product = complex_product(transmission[layer_index], wavefield)
        extended = padded(product, (("tile", 2),), 1)
        wavefield = propagate(extended, PROP_IM)
    return (jnp.stack(inputs, 1), wavefield)


def backward_section(adjoint, inputs, weight, transmission):
    slice_count = transmission.shape[0]
    slice_grads = [None] * slice_count
    scaled = weight[:, None, None, None]
    for layer_index in reversed(range(slice_count)):
        extended = padded(adjoint, (("tile", 2),), 1)
        adjoint_wave = propagate(extended, -PROP_IM)
        slice_grads[layer_index] = jnp.sum(
            scaled * conjugate_product(inputs[:, layer_index], adjoint_wave), 0
        )
        adjoint = conjugate_product(transmission[layer_index], adjoint_wave)
    return (adjoint, jnp.stack(slice_grads, 0))


def body(probe, offsets, phase, absorption, measured):
    slice_count, row_count, col_count = phase.shape
    amplitude = jnp.exp(-absorption)
    transmission = jnp.stack([amplitude * jnp.cos(phase), amplitude * jnp.sin(phase)], 1)
    sections = lax.axis_size("sec")
    section = lax.axis_index("sec")
    probe_count = offsets.shape[0]
    batch_size = 1
    step_count = sections + probe_count - 1

    def plan(step_index, offset_steps):
        raw_ids = (step_index - offset_steps)[None]
        active = (raw_ids >= 0) & (raw_ids < probe_count)
        return (jnp.clip(raw_ids, 0, probe_count - 1), active)

    def launch(shift_amount):
        return jnp.roll(probe, shift_amount, axis=-1)

    def forward_step(step_index, state_carry):
        incoming, stored, exit_waves = state_carry
        probe_ids, active = plan(step_index, section)
        launched = jax.vmap(launch)(offsets[probe_ids])
        wavefield = jnp.where(section == 0, launched, incoming)
        inputs, outgoing = forward_section(wavefield, transmission)
        stored = stored.at[probe_ids].set(
            jnp.where(active[:, None, None, None, None], inputs, stored[probe_ids])
        )
        exit_waves = exit_waves.at[probe_ids].set(
            jnp.where(active[:, None, None, None], outgoing, exit_waves[probe_ids])
        )
        incoming = passed_along(outgoing, "sec", 1)
        return (incoming, stored, exit_waves)

    zero_field = jnp.zeros((batch_size, 2, row_count, col_count), jnp.float32)
    stored = jnp.zeros((probe_count, slice_count, 2, row_count, col_count), jnp.float32)
    exit_waves = jnp.zeros((probe_count, 2, row_count, col_count), jnp.float32)
    unused, stored, exit_waves = lax.fori_loop(
        0, step_count, forward_step, (zero_field, stored, exit_waves)
    )

    def backward_step(step_index, state_carry):
        incoming, gradient = state_carry
        probe_ids, active = plan(step_index, sections - 1 - section)
        exit_part = exit_waves[probe_ids]
        intensity = exit_part[:, 0] ** 2 + exit_part[:, 1] ** 2
        seed_adjoint = 2.0 * (intensity - measured[probe_ids])[:, None] * exit_part
        adjoint = jnp.where(section == sections - 1, seed_adjoint, incoming)
        weight = active.astype(jnp.float32)
        adjoint, gradient_terms = backward_section(adjoint, stored[probe_ids], weight, transmission)
        incoming = passed_along(adjoint, "sec", -1)
        return (incoming, gradient + gradient_terms)

    gradient = jnp.zeros((slice_count, 2, row_count, col_count), jnp.float32)
    unused, gradient = lax.fori_loop(0, step_count, backward_step, (zero_field, gradient))
    return gradient


def solution(mesh):
    in_specs = (
        P(None, "tile", None),
        P(),
        P("sec", "tile", None),
        P("sec", "tile", None),
        P(None, "tile", None),
    )
    out_specs = P("sec", None, "tile", None)
    return jax.shard_map(body, mesh=mesh, in_specs=in_specs, out_specs=out_specs, check_vma=False)
```

profile of v0, /device:TPU:0, one launch (start us, length us, event | category | flops | bytes accessed | tf_op | source)
XLA Modules:
  0.0 785.4 jit_solution(1583866318496950001)
XLA Ops:
  2.4 420.5 %while.46 = (s32[]{:T(128)}, f32[1,2,8,512]{3,2,1,0:T(8,128)S(1)}, f32[4,2,2,8,512]{4,3,2,1,0:T(8,128)S(1)}, f32[4,2,8,512]{3,2,1,0:T(8,128)S(1)}, f32[2,2,8,512...) while((s32[]{:T(128)}, f32[1,2,8,512]{3,2,1,0:T(8,128)S(1)}, ...), condition=%wide.region_3.4_spmd, body=%wide.region_0.3_spmd.sunk | while | flops 438341 | bytes 1737424 | solution.py:136
  6.5 3.0 collective-permute-start.1
  12.8 3.0 collective-permute-start.3
  17.4 4.9 collective-permute-start.4
  28.0 3.0 collective-permute-start.1
  34.2 3.0 collective-permute-start.3
  38.9 4.2 collective-permute-start.4
  55.0 3.0 collective-permute-start.3
  59.7 4.3 collective-permute-start.4
  69.7 3.0 collective-permute-start.1
  80.6 5.1 collective-permute-start.4
  91.4 3.0 collective-permute-start.1
  102.3 5.1 collective-permute-start.4
  113.1 3.0 collective-permute-start.1
  119.3 3.0 collective-permute-start.3
  124.0 5.1 collective-permute-start.4
  141.0 3.0 collective-permute-start.3
  145.7 5.1 collective-permute-start.4
  162.8 3.0 collective-permute-start.3
  167.4 5.3 collective-permute-start.4
  184.6 3.0 collective-permute-start.3
  189.2 6.0 collective-permute-start.4
  200.9 3.0 collective-permute-start.1
  207.2 3.0 collective-permute-start.3
  211.8 6.0 collective-permute-start.4
  229.8 3.0 collective-permute-start.3
  234.4 6.0 collective-permute-start.4
  246.2 3.0 collective-permute-start.1
  252.4 3.0 collective-permute-start.3
  257.1 6.0 collective-permute-start.4
  268.8 3.0 collective-permute-start.1
  275.0 3.0 collective-permute-start.3
  279.7 6.0 collective-permute-start.4
  291.4 3.0 collective-permute-start.1
  297.6 3.0 collective-permute-start.3
  302.3 6.0 collective-permute-start.4
  314.0 3.0 collective-permute-start.1
  324.9 6.0 collective-permute-start.4
  336.6 3.0 collective-permute-start.1
  342.8 3.0 collective-permute-start.3
  347.5 6.0 collective-permute-start.4
  370.1 6.0 collective-permute-start.4
  392.7 6.0 collective-permute-start.4
  415.3 6.0 collective-permute-start.4
  422.9 361.9 %while.47 = (s32[]{:T(128)}, f32[1,2,8,512]{3,2,1,0:T(8,128)S(1)}, f32[2,2,8,512]{3,2,1,0:T(8,128)S(1)}, f32[2,2,8,512]{3,2,1,0:T(8,128)S(1)}, pred[]{:T(512)}, ...) while((s32[]{:T(128)}, f32[1,2,8,512]{3,2,1,0:T(8,128)S(1)}, ...), condition=%wide.region_5.6_spmd.clone, body=%wide.region_4.5_spmd.clone.sunk | while | flops 481291 | bytes 2089406 | solution.py:153
  435.6 6.6 collective-permute-done.9
  454.9 6.6 collective-permute-done.9
  474.2 6.6 collective-permute-done.9
  493.5 6.6 collective-permute-done.9
  512.8 6.3 collective-permute-done.9
  531.8 6.3 collective-permute-done.9
  550.8 6.3 collective-permute-done.9
  569.7 6.3 collective-permute-done.9
  588.7 6.3 collective-permute-done.9
  607.7 6.3 collective-permute-done.9
  626.7 6.3 collective-permute-done.9
  645.7 6.3 collective-permute-done.9
  664.7 6.3 collective-permute-done.9
  683.6 6.3 collective-permute-done.9
  702.6 6.3 collective-permute-done.9
  721.6 6.3 collective-permute-done.9
  740.6 6.3 collective-permute-done.9
  759.6 6.3 collective-permute-done.9
  778.6 6.3 collective-permute-done.9
  (1077 shorter events, 444.1 us)
Async XLA Ops:
  5.2 6.1 collective-permute-start
  6.5 4.8 collective-permute-start.1
  17.4 6.5 collective-permute-start.4
  26.7 6.1 collective-permute-start
  28.0 4.8 collective-permute-start.1
  38.9 5.8 collective-permute-start.4
  47.5 6.1 collective-permute-start
  59.7 5.9 collective-permute-start.4
  68.4 6.1 collective-permute-start
  69.7 4.8 collective-permute-start.1
  80.6 6.7 collective-permute-start.4
  90.1 6.1 collective-permute-start
  91.4 4.8 collective-permute-start.1
  102.3 6.7 collective-permute-start.4
  111.8 6.1 collective-permute-start
  113.1 4.8 collective-permute-start.1
  124.0 6.7 collective-permute-start.4
  133.5 6.1 collective-permute-start
  145.7 6.7 collective-permute-start.4
  155.2 6.1 collective-permute-start
  156.5 4.8 collective-permute-start.1
  167.4 6.9 collective-permute-start.4
  177.0 6.1 collective-permute-start
  189.2 7.6 collective-permute-start.4
  199.6 6.1 collective-permute-start
  200.9 4.8 collective-permute-start.1
  211.8 7.6 collective-permute-start.4
  222.2 6.1 collective-permute-start
  234.4 7.6 collective-permute-start.4
  244.8 6.1 collective-permute-start
  257.1 7.6 collective-permute-start.4
  267.5 6.1 collective-permute-start
  279.7 7.6 collective-permute-start.4
  290.1 6.1 collective-permute-start
  302.3 7.6 collective-permute-start.4
  312.7 6.1 collective-permute-start
  324.9 7.6 collective-permute-start.4
  335.3 6.1 collective-permute-start
  347.5 7.6 collective-permute-start.4
  357.9 6.1 collective-permute-start
  370.1 7.6 collective-permute-start.4
  380.5 6.1 collective-permute-start
  392.7 7.6 collective-permute-start.4
  403.1 6.1 collective-permute-start
  415.3 7.6 collective-permute-start.4
  434.3 7.9 %collective-permute-start.9 = (f32[1,2,8,512]{3,2,1,0:T(8,128)S(1)}, f32[1,2,8,512]{3,2,1,0:T(8,128)S(1)}, u32[]{:S(2)}, u32[]{:S(2)}) collective-permute-start(f32[1,2,8,512]{3,2,1,0:T(8,128)S(1)} %pad_maximum_fusion.22), channel_id=1, source_target_pairs={{2,0},{4,2},{6,4},{8,6},{10,8},{12,10},{14,12},{16,14},{18,16},{20... | collective-permute-start | bytes 98312 | tf_op jit(solution)/shard_map/while/body/eval_jaxpr/ppermute | solution.py:26
  453.6 7.9 %collective-permute-start.9 = (f32[1,2,8,512]{3,2,1,0:T(8,128)S(1)}, f32[1,2,8,512]{3,2,1,0:T(8,128)S(1)}, u32[]{:S(2)}, u32[]{:S(2)}) collective-permute-start(f32[1,2,8,512]{3,2,1,0:T(8,128)S(1)} %pad_maximum_fusion.22), channel_id=1, source_target_pairs={{2,0},{4,2},{6,4},{8,6},{10,8},{12,10},{14,12},{16,14},{18,16},{20... | collective-permute-start | bytes 98312 | tf_op jit(solution)/shard_map/while/body/eval_jaxpr/ppermute | solution.py:26
  472.9 7.9 %collective-permute-start.9 = (f32[1,2,8,512]{3,2,1,0:T(8,128)S(1)}, f32[1,2,8,512]{3,2,1,0:T(8,128)S(1)}, u32[]{:S(2)}, u32[]{:S(2)}) collective-permute-start(f32[1,2,8,512]{3,2,1,0:T(8,128)S(1)} %pad_maximum_fusion.22), channel_id=1, source_target_pairs={{2,0},{4,2},{6,4},{8,6},{10,8},{12,10},{14,12},{16,14},{18,16},{20... | collective-permute-start | bytes 98312 | tf_op jit(solution)/shard_map/while/body/eval_jaxpr/ppermute | solution.py:26
  492.2 7.9 %collective-permute-start.9 = (f32[1,2,8,512]{3,2,1,0:T(8,128)S(1)}, f32[1,2,8,512]{3,2,1,0:T(8,128)S(1)}, u32[]{:S(2)}, u32[]{:S(2)}) collective-permute-start(f32[1,2,8,512]{3,2,1,0:T(8,128)S(1)} %pad_maximum_fusion.22), channel_id=1, source_target_pairs={{2,0},{4,2},{6,4},{8,6},{10,8},{12,10},{14,12},{16,14},{18,16},{20... | collective-permute-start | bytes 98312 | tf_op jit(solution)/shard_map/while/body/eval_jaxpr/ppermute | solution.py:26
  511.4 7.6 collective-permute-start.9
  530.4 7.6 collective-permute-start.9
  549.4 7.6 collective-permute-start.9
  568.4 7.6 collective-permute-start.9
  587.4 7.6 collective-permute-start.9
  606.4 7.6 collective-permute-start.9
  625.3 7.6 collective-permute-start.9
  644.3 7.6 collective-permute-start.9
  663.3 7.6 collective-permute-start.9
  682.3 7.6 collective-permute-start.9
  701.3 7.6 collective-permute-start.9
  720.3 7.6 collective-permute-start.9
  739.2 7.6 collective-permute-start.9
  758.2 7.6 collective-permute-start.9
  777.2 7.6 collective-permute-start.9
  (131 other events, 532.6 us)
where the time goes:
time: 800 us; the launch traced here: 785 us
  starting transfers between devices  458 us (57%)
  waiting for transfers between devices  177 us (22%)
  other arithmetic  88.5 us (11%)
  loops' own time  43 us (5%)
  local copies, waits for them, and re-layouts  19 us (2%)
    ppermute x76, starting transfers between devices, padded(): before = lax.ppermute(last, axis, up)  230 us
    ppermute x38, waiting for transfers between devices, passed_along(): lax.ppermute(value, axis, [(source, source + steps) for source in range(i...  137 us
    ppermute x38, starting transfers between devices, passed_along(): lax.ppermute(value, axis, [(source, source + steps) for source in range(i...  130 us
    ppermute x76, starting transfers between devices, padded(): after = lax.ppermute(initial, axis, down)  98.2 us
    another operation x1, loops' own time, body(): lax.fori_loop(0, step_count, forward_step, (zero_field, stored, exit_waves))  40.7 us
    ppermute x76, waiting for transfers between devices, padded(): before = lax.ppermute(last, axis, up)  39.6 us
    another operation x38, other arithmetic  28.2 us
  transfers between devices with their start and end apart: 190, of which 95 were waited for; matrix products, arithmetic and copies ran while one was open for 7% of the time, Pallas kernels for 0%

commit v1 on v0

--- a/solution.py
+++ b/solution.py
@@ -1,6 +1,10 @@
+import functools
+
 import jax
 import jax.numpy as jnp
 from jax import lax
+from jax.experimental import pallas as pl
+from jax.experimental.pallas import tpu as pltpu
 from jax.sharding import PartitionSpec as P
 
 PROP_RE = 0.004
@@ -97,7 +101,7 @@
     return (adjoint, jnp.stack(slice_grads, 0))
 
 
-def body(probe, offsets, phase, absorption, measured):
+def pipelined_body(probe, offsets, phase, absorption, measured):
     slice_count, row_count, col_count = phase.shape
     amplitude = jnp.exp(-absorption)
     transmission = jnp.stack([amplitude * jnp.cos(phase), amplitude * jnp.sin(phase)], 1)
@@ -154,6 +158,335 @@
     return gradient
 
 
+LANES = 128
+SUBLANES = 8
+MESH = pl.DeviceIdType.MESH
+CENTRE_RE = 1.0 - 4.0 * PROP_RE
+CENTRE_IM = -4.0 * PROP_IM
+RATIO = complex(PROP_RE, PROP_IM) / complex(CENTRE_RE, CENTRE_IM)
+
+
+def windowed(sections, tiles, slice_count, row_count, col_count, probe_count):
+    groups = col_count // LANES
+    return (
+        col_count % LANES == 0
+        and groups >= 2
+        and groups % 2 == 0
+        and sections % groups == 0
+        and row_count % SUBLANES == 0
+        and probe_count % tiles == 0
+        and 2 * sections * slice_count <= LANES // 2
+        and tiles * row_count <= 4 * SUBLANES
+    )
+
+
+def window_kernel(
+    sections, tiles,
+    probe_ref, offsets_ref, phase_ref, absorption_ref, measured_ref, out_ref,
+    own, field, probes, frames, waves, adjoint, partial, returned,
+    group_send, block_recv, plane_send, tile_send, tile_recv,
+    aux_send, aux_recv, back_send, back_recv,
+):
+    slice_count, row_count, col_count = phase_ref.shape
+    groups = col_count // LANES
+    plane = sections // groups
+    width = 2 * LANES
+    height = tiles * row_count
+    share = frames.shape[1]
+    me = lax.axis_index("sec")
+    tile = lax.axis_index("tile")
+    group, place = lax.div(me, plane), lax.rem(me, plane)
+    sent = []
+
+    def device(section, core):
+        return {"sec": section, "tile": core}
+
+    def group_at(step):
+        return lax.rem(group + step, groups)
+
+    def place_at(step):
+        return lax.rem(place + step, plane)
+
+    def tile_at(step):
+        return lax.rem(tile + step, tiles)
+
+    def send(source, target, send_sem, recv_sem, section, core):
+        copy = pltpu.make_async_remote_copy(
+            src_ref=source, dst_ref=target, send_sem=send_sem, recv_sem=recv_sem,
+            device_id=device(section, core), device_id_type=MESH,
+        )
+        copy.start()
+        sent.append(copy)
+
+    def arrived(target, recv_sem):
+        pltpu.make_async_remote_copy(
+            src_ref=target, dst_ref=target, send_sem=recv_sem, recv_sem=recv_sem,
+            device_id=device(me, tile), device_id_type=MESH,
+        ).wait_recv()
+
+    barrier = pltpu.get_barrier_semaphore()
+    partners = 0
+    for dz in range(groups):
+        for dj in range(tiles):
+            if dz or dj:
+                pl.semaphore_signal(
+                    barrier, inc=1, device_id=device(group_at(dz) * plane + place, tile_at(dj)),
+                    device_id_type=MESH,
+                )
+                partners += 1
+    for dq in range(1, plane):
+        pl.semaphore_signal(
+            barrier, inc=1, device_id=device(group * plane + place_at(dq), tile), device_id_type=MESH
+        )
+        partners += 1
+
+    for layer in range(slice_count):
+        amplitude = jnp.exp(-absorption_ref[layer])
+        real = amplitude * jnp.cos(phase_ref[layer])
+        imag = amplitude * jnp.sin(phase_ref[layer])
+        for part, value in enumerate(
+            (CENTRE_RE * real - CENTRE_IM * imag, CENTRE_RE * imag + CENTRE_IM * real)
+        ):
+            own[layer, part, :, :col_count] = value
+            own[layer, part, :, col_count:] = value[:, :LANES]
+    start = pl.multiple_of(group * LANES, LANES)
+    field[me, tile] = own[:, :, :, pl.ds(start, width)]
+    probes[tile] = probe_ref[...]
+    frames[tile] = measured_ref[pl.ds(tile * share, share)]
+    pl.semaphore_wait(barrier, partners)
+
+    step = 1 - 2 * lax.div(2 * group, groups)
+    near = [lax.rem(group + dz * step + groups, groups) for dz in range(groups)]
+    for dz in range(groups - 1, 0, -1):
+        target = near[dz]
+        window = pl.ds(pl.multiple_of(target * LANES, LANES), width)
+        send(
+            own.at[:, :, :, window], field.at[me, tile], group_send.at[dz], block_recv.at[me],
+            target * plane + place, tile,
+        )
+
+    def to_plane(dz):
+        block = near[dz] * plane + place
+        for dq in range(1, plane):
+            send(
+                field.at[block, tile], field.at[block, tile], plane_send.at[dz, dq],
+                block_recv.at[block], group * plane + place_at(dq), tile,
+            )
+
+    def to_tiles(block, dz, dq):
+        for dj in range(1, tiles):
+            send(
+                field.at[block, tile], field.at[block, tile], tile_send.at[dz, dq, dj],
+                tile_recv.at[block, tile], me, tile_at(dj),
+            )
+
+    to_plane(0)
+    for dj in range(1, tiles):
+        other = tile_at(dj)
+        send(probe_ref, probes.at[tile], aux_send.at[0, dj], aux_recv.at[0, tile], me, other)
+        send(
+            measured_ref.at[pl.ds(other * share, share)], frames.at[tile], aux_send.at[1, dj],
+            aux_recv.at[1, tile], me, other,
+        )
+    to_tiles(me, 0, 0)
+
+    for dj in range(1, tiles):
+        other = tile_at(dj)
+        arrived(probes.at[other], aux_recv.at[0, other])
+        arrived(frames.at[other], aux_recv.at[1, other])
+    for index in range(share):
+        shift = lax.rem(
+            offsets_ref[tile * share + index] + col_count - group * LANES, col_count
+        )
+        for part in range(2):
+            value = jnp.concatenate([probes[t, part] for t in range(tiles)], 0)
+            for bit in range((col_count - 1).bit_length()):
+                chosen = jnp.full(value.shape, lax.shift_right_logical(shift, bit) & 1) == 1
+                value = jnp.where(chosen, pltpu.roll(value, 1 << bit, 1), value)
+            waves[0, index, part] = value[:, :width]
+
+    def collect(dz):
+        for dq in range(1, plane):
+            block = near[dz] * plane + place_at(dq)
+            arrived(field.at[block, tile], block_recv.at[block])
+            to_tiles(block, dz, dq)
+
+    for dz in range(1, groups):
+        block = near[dz] * plane + place
+        arrived(field.at[block, tile], block_recv.at[block])
+        to_plane(dz)
+        to_tiles(block, dz, 0)
+        collect(dz - 1)
+    collect(groups - 1)
+
+    rows = lax.broadcasted_iota(jnp.int32, (height, width), 0)
+    first, last = rows == 0, rows == height - 1
+
+    def neighbours(value):
+        above = jnp.where(first, 0.0, pltpu.roll(value, 1, 0))
+        below = jnp.where(last, 0.0, pltpu.roll(value, height - 1, 0))
+        return (above + below) + (pltpu.roll(value, 1, 1) + pltpu.roll(value, width - 1, 1))
+
+    def spread(real, imag, ratio):
+        real_sum, imag_sum = neighbours(real), neighbours(imag)
+        return (
+            real + (ratio.real * real_sum - ratio.imag * imag_sum),
+            imag + (ratio.real * imag_sum + ratio.imag * real_sum),
+        )
+
+    def layer_of(block, layer):
+        return [
+            jnp.concatenate([field[block, t, layer, part] for t in range(tiles)], 0)
+            for part in range(2)
+        ]
+
+    def forward(block, carry):
+        for dj in range(1, tiles):
+            other = tile_at(dj)
+            arrived(field.at[block, other], tile_recv.at[block, other])
+        for layer in range(slice_count):
+            at = block * slice_count + layer
+            real, imag = layer_of(block, layer)
+            for index in range(share):
+                wave_re, wave_im = waves[at, index, 0], waves[at, index, 1]
+                wave_re, wave_im = spread(
+                    real * wave_re - imag * wave_im, real * wave_im + imag * wave_re, RATIO
+                )
+                waves[at + 1, index, 0] = wave_re
+                waves[at + 1, index, 1] = wave_im
+        return carry
+
+    lax.fori_loop(0, sections, forward, 0)
+
+    following = pl.multiple_of(group_at(1) * LANES, LANES)
+    for index in range(share):
+        frame = jnp.concatenate(
+            [
+                jnp.concatenate([frames[t, index, :, pl.ds(at, LANES)] for t in range(tiles)], 0)
+                for at in (start, following)
+            ],
+            1,
+        )
+        wave_re, wave_im = (waves[sections * slice_count, index, part] for part in range(2))
+        residual = 2.0 * (wave_re * wave_re + wave_im * wave_im - frame)
+        adjoint[index, 0] = residual * wave_re
+        adjoint[index, 1] = residual * wave_im
+
+    def return_copy(piece, core):
+        return pltpu.make_async_remote_copy(
+            src_ref=partial.at[piece, core], dst_ref=returned.at[group, tile],
+            send_sem=back_send.at[piece, core], recv_sem=back_recv.at[group, tile],
+            device_id=device(piece * plane + place, core), device_id_type=MESH,
+        )
+
+    def backward(count, carry):
+        block = sections - 1 - count
+        piece = lax.div(block, plane)
+        wanted = lax.rem(block, plane) == place
+        for layer in reversed(range(slice_count)):
+            at = block * slice_count + layer
+            real, imag = layer_of(block, layer)
+            backs = []
+            for index in range(share):
+                back_re, back_im = spread(adjoint[index, 0], adjoint[index, 1], RATIO.conjugate())
+                backs.append((back_re, back_im))
+                adjoint[index, 0] = real * back_re + imag * back_im
+                adjoint[index, 1] = real * back_im - imag * back_re
+
+            @pl.when(wanted)
+            def _():
+                total_re = total_im = 0.0
+                for index, (back_re, back_im) in enumerate(backs):
+                    wave_re, wave_im = waves[at, index, 0], waves[at, index, 1]
+                    total_re += wave_re * back_re + wave_im * back_im
+                    total_im += wave_re * back_im - wave_im * back_re
+                for part, total in enumerate((total_re, total_im)):
+                    chunk = pltpu.roll(total, width - LANES // 2, 1)[:, :LANES]
+                    for core in range(tiles):
+                        partial[piece, core, layer, part] = chunk[
+                            core * row_count : (core + 1) * row_count
+                        ]
+
+        for core in range(tiles):
+            @pl.when(wanted & (piece * tiles + core != group * tiles + tile))
+            def _():
+                return_copy(piece, core).start()
+
+        return carry
+
+    lax.fori_loop(0, sections - place, backward, 0)
+
+    returned[group, tile] = partial[group, tile]
+    for dz in range(groups):
+        for dj in range(tiles):
+            if dz or dj:
+                piece, core = group_at(dz), tile_at(dj)
+                arrived(returned.at[piece, core], back_recv.at[piece, core])
+    for layer in range(slice_count):
+        parts = []
+        for part in range(2):
+            chunks = []
+            for piece in range(groups):
+                chunk = returned[piece, 0, layer, part]
+                for core in range(1, tiles):
+                    chunk = chunk + returned[piece, core, layer, part]
+                chunks.append(chunk)
+            parts.append(pltpu.roll(jnp.concatenate(chunks, 1), LANES // 2, 1))
+        real, imag = parts
+        out_ref[layer, 0] = CENTRE_RE * real + CENTRE_IM * imag
+        out_ref[layer, 1] = CENTRE_RE * imag - CENTRE_IM * real
+
+    for dz in range(groups):
+        for dj in range(tiles):
+            if dz or dj:
+                return_copy(group_at(dz), tile_at(dj)).wait_send()
+    for copy in sent:
+        copy.wait_send()
+
+
+def windowed_body(sections, tiles, probe, offsets, phase, absorption, measured):
+    slice_count, row_count, col_count = phase.shape
+    probe_count = offsets.shape[0]
+    groups = col_count // LANES
+    plane = sections // groups
+    width, height, share = 2 * LANES, tiles * row_count, probe_count // tiles
+    vmem = pl.BlockSpec(memory_space=pltpu.VMEM)
+    dma = pltpu.SemaphoreType.DMA
+    return pl.pallas_call(
+        functools.partial(window_kernel, sections, tiles),
+        out_shape=jax.ShapeDtypeStruct((slice_count, 2, row_count, col_count), jnp.float32),
+        in_specs=[vmem, pl.BlockSpec(memory_space=pltpu.SMEM), vmem, vmem, vmem],
+        out_specs=vmem,
+        scratch_shapes=[
+            pltpu.VMEM((slice_count, 2, row_count, col_count + LANES), jnp.float32),
+            pltpu.VMEM((sections, tiles, slice_count, 2, row_count, width), jnp.float32),
+            pltpu.VMEM((tiles, 2, row_count, col_count), jnp.float32),
+            pltpu.VMEM((tiles, share, row_count, col_count), jnp.float32),
+            pltpu.VMEM((sections * slice_count + 1, share, 2, height, width), jnp.float32),
+            pltpu.VMEM((share, 2, height, width), jnp.float32),
+            pltpu.VMEM((groups, tiles, slice_count, 2, row_count, LANES), jnp.float32),
+            pltpu.VMEM((groups, tiles, slice_count, 2, row_count, LANES), jnp.float32),
+            dma((groups,)),
+            dma((sections,)),
+            dma((groups, plane)),
+            dma((groups, plane, tiles)),
+            dma((sections, tiles)),
+            dma((2, tiles)),
+            dma((2, tiles)),
+            dma((groups, tiles)),
+            dma((groups, tiles)),
+        ],
+        compiler_params=pltpu.CompilerParams(collective_id=0, has_side_effects=True),
+    )(probe, offsets, phase, absorption, measured)
+
+
+def body(probe, offsets, phase, absorption, measured):
+    sections, tiles = lax.axis_size("sec"), lax.axis_size("tile")
+    if windowed(sections, tiles, *phase.shape, offsets.shape[0]):
+        return windowed_body(sections, tiles, probe, offsets, phase, absorption, measured)
+    return pipelined_body(probe, offsets, phase, absorption, measured)
+
+
 def solution(mesh):
     in_specs = (
         P(None, "tile", None),

time: 800 us -> 32.6 us (0.04); the launches traced: 785 us -> 32.4 us
  starting transfers between devices: 458 us -> 0 us
  waiting for transfers between devices: 177 us -> 0 us
  other arithmetic: 88.5 us -> 0 us
  loops' own time: 43 us -> 0 us
  Pallas kernels: 0 us -> 30.9 us
  local copies, waits for them, and re-layouts: 19 us -> 1.47 us
    ppermute x190 -> x0, starting transfers between devices: 458 us -> none  [the longest x76 230 us: padded(): before = lax.ppermute(last, axis, up)]
    ppermute x190 -> x0, waiting for transfers between devices: 177 us -> none  [the longest x38 137 us: passed_along(): lax.ppermute(value, axis, [(source, source + steps) for source in range(i...]
    another operation x2 -> x0, loops' own time: 43 us -> none  [the longest x1 40.7 us: body(): lax.fori_loop(0, step_count, forward_step, (zero_field, stored, exit_waves))]
    another operation x249 -> x0, other arithmetic: 38 us -> none
    pallas_call x0 -> x1, Pallas kernels: none -> 30.9 us  [windowed_body(): pl.pallas_call(functools.partial(window_kernel, sections, tiles), out_sha...]
    scatter x38 -> x0, other arithmetic: 26.1 us -> none  [the longest x19 13.1 us: forward_step(): exit_waves.at[probe_ids]]
    mul x57 -> x0, other arithmetic: 14.1 us -> none  [the longest x19 13.8 us: backward_step(): seed_adjoint = 2.0 * (intensity - measured[probe_ids])[:, None] * exit_part]
    gather x19 -> x0, local copies, waits for them, and re-layouts: 12.3 us -> none  [forward_step(): launched = jax.vmap(launch)(offsets[probe_ids])]
  transfers between devices with their start and end apart: 190 -> 0, of which waited for: 95 -> 0; matrix products, arithmetic and copies ran while one was open for 7% -> 0% of each run, Pallas kernels for 0% -> 0%
where the time goes in v1:
time: 32.6 us; the launch traced here: 32.4 us
  Pallas kernels  30.9 us (95%)
  local copies, waits for them, and re-layouts  1.47 us (5%)
    pallas_call x1, Pallas kernels, windowed_body(): pl.pallas_call(functools.partial(window_kernel, sections, tiles), out_sha...  30.9 us
    unnamed x1, local copies, waits for them, and re-layouts  1.47 us

profile of v1, /device:TPU:0, one launch (start us, length us, event | category | flops | bytes accessed | tf_op | source)
XLA Modules:
  0.0 32.4 jit_solution(1381600902988187713)
XLA Ops:
  0.0 30.9 %shard_map.55 = f32[2,2,8,512]{3,2,1,0:T(8,128)} custom-call(f32[2,8,512]{2,1,0:T(8,128)} %probe_ref.1, s32[4]{0:T(128)} %offsets_ref.1, f32[2,8,512]{2,1,0:T(8,128)} %phase_ref.1, f32[2,8,512]{2,1,0:T(8,128)} %absorption_ref.1, f32[4,8,512]{2,1,0:T(8,128)} %measured_ref.1), custom_call_target="tpu_custom_call" | custom-call | tf_op jit(solution)/shard_map/pallas_call | solution.py:455
  31.0 1.5 %copy.7 = f32[2,2,8,512]{3,2,1,0:T(8,128)} copy(f32[2,2,8,512]{3,2,1,0:T(8,128)} %shard_map.55) | data formatting | bytes 131072

commit v2 on v1

--- a/solution.py
+++ b/solution.py
@@ -172,7 +172,7 @@
         col_count % LANES == 0
         and groups >= 2
         and groups % 2 == 0
-        and sections % groups == 0
+        and sections == 4 * groups
         and row_count % SUBLANES == 0
         and probe_count % tiles == 0
         and 2 * sections * slice_count <= LANES // 2
@@ -183,9 +183,9 @@
 def window_kernel(
     sections, tiles,
     probe_ref, offsets_ref, phase_ref, absorption_ref, measured_ref, out_ref,
-    own, field, probes, frames, waves, adjoint, partial, returned,
-    group_send, block_recv, plane_send, tile_send, tile_recv,
-    aux_send, aux_recv, back_send, back_recv,
+    chain, field, probes, frames, waves, adjoint, partial, returned, shifts,
+    chain_send, chain_recv, plane_send, block_recv, corner_send, corner_recv,
+    tile_send, tile_recv, aux_send, aux_recv, back_send, back_recv, shift_sem,
 ):
     slice_count, row_count, col_count = phase_ref.shape
     groups = col_count // LANES
@@ -196,7 +196,8 @@
     me = lax.axis_index("sec")
     tile = lax.axis_index("tile")
     group, place = lax.div(me, plane), lax.rem(me, plane)
-    sent = []
+    across = (place + 1 - 2 * lax.rem(place, 2), place + 2 - 4 * lax.div(place, 2))
+    corner = plane - 1 - place
 
     def device(section, core):
         return {"sec": section, "tile": core}
@@ -204,41 +205,34 @@
     def group_at(step):
         return lax.rem(group + step, groups)
 
-    def place_at(step):
-        return lax.rem(place + step, plane)
-
     def tile_at(step):
         return lax.rem(tile + step, tiles)
 
-    def send(source, target, send_sem, recv_sem, section, core):
-        copy = pltpu.make_async_remote_copy(
+    def remote(source, target, send_sem, recv_sem, section, core):
+        return pltpu.make_async_remote_copy(
             src_ref=source, dst_ref=target, send_sem=send_sem, recv_sem=recv_sem,
             device_id=device(section, core), device_id_type=MESH,
         )
-        copy.start()
-        sent.append(copy)
 
     def arrived(target, recv_sem):
-        pltpu.make_async_remote_copy(
-            src_ref=target, dst_ref=target, send_sem=recv_sem, recv_sem=recv_sem,
-            device_id=device(me, tile), device_id_type=MESH,
-        ).wait_recv()
-
-    barrier = pltpu.get_barrier_semaphore()
-    partners = 0
-    for dz in range(groups):
-        for dj in range(tiles):
-            if dz or dj:
-                pl.semaphore_signal(
-                    barrier, inc=1, device_id=device(group_at(dz) * plane + place, tile_at(dj)),
-                    device_id_type=MESH,
-                )
-                partners += 1
-    for dq in range(1, plane):
+        remote(target, target, recv_sem, recv_sem, me, tile).wait_recv()
+
+    shift_copy = pltpu.make_async_copy(offsets_ref, shifts, shift_sem)
+    shift_copy.start()
+
+    def greet(section, core):
         pl.semaphore_signal(
-            barrier, inc=1, device_id=device(group * plane + place_at(dq), tile), device_id_type=MESH
-        )
-        partners += 1
+            pltpu.get_barrier_semaphore(), inc=1, device_id=device(section, core), device_id_type=MESH
+        )
+
+    for direction in (1, -1):
+        @pl.when((group + direction >= 0) & (group + direction < groups))
+        def _():
+            greet(me + direction * plane, tile)
+    for other in across:
+        greet(group * plane + other, tile)
+    for dj in range(1, tiles):
+        greet(me, tile_at(dj))
 
     for layer in range(slice_count):
         amplitude = jnp.exp(-absorption_ref[layer])
@@ -247,77 +241,132 @@
         for part, value in enumerate(
             (CENTRE_RE * real - CENTRE_IM * imag, CENTRE_RE * imag + CENTRE_IM * real)
         ):
-            own[layer, part, :, :col_count] = value
-            own[layer, part, :, col_count:] = value[:, :LANES]
-    start = pl.multiple_of(group * LANES, LANES)
-    field[me, tile] = own[:, :, :, pl.ds(start, width)]
+            chain[group, layer, part, :, :col_count] = value
+            chain[group, layer, part, :, col_count:] = value[:, :LANES]
     probes[tile] = probe_ref[...]
     frames[tile] = measured_ref[pl.ds(tile * share, share)]
-    pl.semaphore_wait(barrier, partners)
-
-    step = 1 - 2 * lax.div(2 * group, groups)
-    near = [lax.rem(group + dz * step + groups, groups) for dz in range(groups)]
-    for dz in range(groups - 1, 0, -1):
-        target = near[dz]
-        window = pl.ds(pl.multiple_of(target * LANES, LANES), width)
-        send(
-            own.at[:, :, :, window], field.at[me, tile], group_send.at[dz], block_recv.at[me],
-            target * plane + place, tile,
-        )
-
-    def to_plane(dz):
-        block = near[dz] * plane + place
-        for dq in range(1, plane):
-            send(
-                field.at[block, tile], field.at[block, tile], plane_send.at[dz, dq],
-                block_recv.at[block], group * plane + place_at(dq), tile,
+    ends = lax.div(group + groups - 1, groups) + lax.div(2 * groups - 2 - group, groups)
+    pl.semaphore_wait(pltpu.get_barrier_semaphore(), tiles - 1 + len(across) + ends)
+
+    def span(at, direction):
+        return pl.ds((at + 1) * LANES, (groups - at) * LANES) if direction > 0 else pl.ds(0, (at + 1) * LANES)
+
+    def hop(source, at, direction):
+        part = chain.at[source, :, :, :, span(at, direction)]
+        return remote(
+            part, part, chain_send.at[source, (direction + 1) // 2], chain_recv.at[source],
+            me + direction * plane, tile,
+        )
+
+    def hops(at):
+        for source in range(groups):
+            if source <= at < groups - 1:
+                yield hop(source, at, 1)
+            if source >= at > 0:
+                yield hop(source, at, -1)
+
+    def plane_copy(source, view, axis):
+        block = source * plane + place
+        return remote(
+            view, field.at[block, tile], plane_send.at[source, axis], block_recv.at[block],
+            group * plane + across[axis], tile,
+        )
+
+    def corner_copy(source, axis):
+        part = field.at[source * plane + across[axis], tile, :, axis]
+        return remote(
+            part, part, corner_send.at[source, axis], corner_recv.at[source, axis],
+            group * plane + across[1 - axis], tile,
+        )
+
+    def tile_copies(block, view):
+        return [
+            remote(
+                view, field.at[block, tile], tile_send.at[block, dj], tile_recv.at[block, tile],
+                me, tile_at(dj),
             )
-
-    def to_tiles(block, dz, dq):
+            for dj in range(1, tiles)
+        ]
+
+    def aux_copies():
         for dj in range(1, tiles):
-            send(
-                field.at[block, tile], field.at[block, tile], tile_send.at[dz, dq, dj],
-                tile_recv.at[block, tile], me, tile_at(dj),
+            other = tile_at(dj)
+            yield remote(
+                probe_ref, probes.at[tile], aux_send.at[0, dj], aux_recv.at[0, tile], me, other
             )
-
-    to_plane(0)
-    for dj in range(1, tiles):
-        other = tile_at(dj)
-        send(probe_ref, probes.at[tile], aux_send.at[0, dj], aux_recv.at[0, tile], me, other)
-        send(
-            measured_ref.at[pl.ds(other * share, share)], frames.at[tile], aux_send.at[1, dj],
-            aux_recv.at[1, tile], me, other,
-        )
-    to_tiles(me, 0, 0)
-
-    for dj in range(1, tiles):
-        other = tile_at(dj)
-        arrived(probes.at[other], aux_recv.at[0, other])
-        arrived(frames.at[other], aux_recv.at[1, other])
-    for index in range(share):
-        shift = lax.rem(
-            offsets_ref[tile * share + index] + col_count - group * LANES, col_count
-        )
-        for part in range(2):
-            value = jnp.concatenate([probes[t, part] for t in range(tiles)], 0)
-            for bit in range((col_count - 1).bit_length()):
-                chosen = jnp.full(value.shape, lax.shift_right_logical(shift, bit) & 1) == 1
-                value = jnp.where(chosen, pltpu.roll(value, 1 << bit, 1), value)
-            waves[0, index, part] = value[:, :width]
-
-    def collect(dz):
-        for dq in range(1, plane):
-            block = near[dz] * plane + place_at(dq)
-            arrived(field.at[block, tile], block_recv.at[block])
-            to_tiles(block, dz, dq)
-
-    for dz in range(1, groups):
-        block = near[dz] * plane + place
-        arrived(field.at[block, tile], block_recv.at[block])
-        to_plane(dz)
-        to_tiles(block, dz, 0)
-        collect(dz - 1)
-    collect(groups - 1)
+            yield remote(
+                measured_ref.at[pl.ds(other * share, share)], frames.at[tile], aux_send.at[1, dj],
+                aux_recv.at[1, tile], me, other,
+            )
+
+    def launch():
+        for dj in range(1, tiles):
+            other = tile_at(dj)
+            arrived(probes.at[other], aux_recv.at[0, other])
+            arrived(frames.at[other], aux_recv.at[1, other])
+        shift_copy.wait()
+        for index in range(share):
+            shift = lax.rem(shifts[tile * share + index] + col_count - group * LANES, col_count)
+            for part in range(2):
+                value = jnp.concatenate([probes[t, part] for t in range(tiles)], 0)
+                for bit in range((col_count - 1).bit_length()):
+                    chosen = jnp.full(value.shape, lax.shift_right_logical(shift, bit) & 1) == 1
+                    value = jnp.where(chosen, pltpu.roll(value, 1 << bit, 1), value)
+                waves[0, index, part] = value[:, :width]
+
+    def gather(at):
+        window = pl.ds(at * LANES, width)
+        order = sorted(range(groups), key=lambda source: (abs(source - at), source))
+
+        def spread_out(source):
+            if source <= at < groups - 1:
+                hop(source, at, 1).start()
+            if source >= at > 0:
+                hop(source, at, -1).start()
+            view = chain.at[source, :, :, :, window]
+            for axis in range(2):
+                plane_copy(source, view, axis).start()
+            for copy in tile_copies(source * plane + place, view):
+                copy.start()
+            field[source * plane + place, tile] = chain[source, :, :, :, window]
+
+        def collect(source):
+            for axis in range(2):
+                block = source * plane + across[axis]
+                arrived(field.at[block, tile], block_recv.at[block])
+                corner_copy(source, axis).start()
+                for copy in tile_copies(block, field.at[block, tile]):
+                    copy.start()
+
+        def collect_corner(source):
+            block = source * plane + corner
+            for axis in range(2):
+                arrived(field.at[block, tile, :, axis], corner_recv.at[source, axis])
+            for copy in tile_copies(block, field.at[block, tile]):
+                copy.start()
+
+        for count in range(groups + 2):
+            if count < groups:
+                source = order[count]
+                if source < at:
+                    arrived(chain.at[source, :, :, :, span(at - 1, 1)], chain_recv.at[source])
+                if source > at:
+                    arrived(chain.at[source, :, :, :, span(at + 1, -1)], chain_recv.at[source])
+                spread_out(source)
+            if count == 0:
+                for copy in aux_copies():
+                    copy.start()
+            if 0 <= count - 1 < groups:
+                collect(order[count - 1])
+            if 0 <= count - 2 < groups:
+                collect_corner(order[count - 2])
+            if count == 0:
+                launch()
+
+    for at in range(groups):
+        @pl.when(group == at)
+        def _():
+            gather(at)
 
     rows = lax.broadcasted_iota(jnp.int32, (height, width), 0)
     first, last = rows == 0, rows == height - 1
@@ -358,6 +407,7 @@
 
     lax.fori_loop(0, sections, forward, 0)
 
+    start = pl.multiple_of(group * LANES, LANES)
     following = pl.multiple_of(group_at(1) * LANES, LANES)
     for index in range(share):
         frame = jnp.concatenate(
@@ -440,7 +490,19 @@
         for dj in range(tiles):
             if dz or dj:
                 return_copy(group_at(dz), tile_at(dj)).wait_send()
-    for copy in sent:
+    for at in range(groups):
+        @pl.when(group == at)
+        def _():
+            for copy in hops(at):
+                copy.wait_send()
+    for source in range(groups):
+        for axis in range(2):
+            plane_copy(source, field.at[source * plane + place, tile], axis).wait_send()
+            corner_copy(source, axis).wait_send()
+    for block in range(sections):
+        for copy in tile_copies(block, field.at[block, tile]):
+            copy.wait_send()
+    for copy in aux_copies():
         copy.wait_send()
 
 
@@ -455,10 +517,10 @@
     return pl.pallas_call(
         functools.partial(window_kernel, sections, tiles),
         out_shape=jax.ShapeDtypeStruct((slice_count, 2, row_count, col_count), jnp.float32),
-        in_specs=[vmem, pl.BlockSpec(memory_space=pltpu.SMEM), vmem, vmem, vmem],
+        in_specs=[vmem, pl.BlockSpec(memory_space=pl.ANY), vmem, vmem, vmem],
         out_specs=vmem,
         scratch_shapes=[
-            pltpu.VMEM((slice_count, 2, row_count, col_count + LANES), jnp.float32),
+            pltpu.VMEM((groups, slice_count, 2, row_count, col_count + LANES), jnp.float32),
             pltpu.VMEM((sections, tiles, slice_count, 2, row_count, width), jnp.float32),
             pltpu.VMEM((tiles, 2, row_count, col_count), jnp.float32),
             pltpu.VMEM((tiles, share, row_count, col_count), jnp.float32),
@@ -466,15 +528,20 @@
             pltpu.VMEM((share, 2, height, width), jnp.float32),
             pltpu.VMEM((groups, tiles, slice_count, 2, row_count, LANES), jnp.float32),
             pltpu.VMEM((groups, tiles, slice_count, 2, row_count, LANES), jnp.float32),
+            pltpu.SMEM((probe_count,), jnp.int32),
+            dma((groups, 2)),
             dma((groups,)),
+            dma((groups, 2)),
             dma((sections,)),
-            dma((groups, plane)),
-            dma((groups, plane, tiles)),
+            dma((groups, 2)),
+            dma((groups, 2)),
+            dma((sections, tiles)),
             dma((sections, tiles)),
             dma((2, tiles)),
             dma((2, tiles)),
             dma((groups, tiles)),
             dma((groups, tiles)),
+            dma,
         ],
         compiler_params=pltpu.CompilerParams(collective_id=0, has_side_effects=True),
     )(probe, offsets, phase, absorption, measured)

time: 32.6 us -> 35.4 us (1.086)
  Pallas kernels: 30.9 us -> 33.7 us
    pallas_call x1, Pallas kernels: 30.9 us -> 33.7 us  [windowed_body(): pl.pallas_call(functools.partial(window_kernel, sections, tiles), out_sha...]
where the time goes in v2:
time: 35.4 us; the launch traced here: 35.2 us
  Pallas kernels  33.7 us (95%)
  local copies, waits for them, and re-layouts  1.47 us (4%)
    pallas_call x1, Pallas kernels, windowed_body(): pl.pallas_call(functools.partial(window_kernel, sections, tiles), out_sha...  33.7 us
    unnamed x1, local copies, waits for them, and re-layouts  1.47 us

profile of v2, /device:TPU:0, one launch (start us, length us, event | category | flops | bytes accessed | tf_op | source)
XLA Modules:
  0.0 35.2 jit_solution(16285028671477636121)
XLA Ops:
  0.0 33.7 %shard_map.55 = f32[2,2,8,512]{3,2,1,0:T(8,128)} custom-call(f32[2,8,512]{2,1,0:T(8,128)} %probe_ref.1, s32[4]{0:T(128)} %offsets_ref.1, f32[2,8,512]{2,1,0:T(8,128)} %phase_ref.1, f32[2,8,512]{2,1,0:T(8,128)} %absorption_ref.1, f32[4,8,512]{2,1,0:T(8,128)} %measured_ref.1), custom_call_target="tpu_custom_call" | custom-call | tf_op jit(solution)/shard_map/pallas_call | solution.py:517
  33.7 1.5 %copy.7 = f32[2,2,8,512]{3,2,1,0:T(8,128)} copy(f32[2,2,8,512]{3,2,1,0:T(8,128)} %shard_map.55) | data formatting | bytes 131072

commit v3 on v2

--- a/solution.py
+++ b/solution.py
@@ -160,6 +160,7 @@
 
 LANES = 128
 SUBLANES = 8
+DIRECT = 2
 MESH = pl.DeviceIdType.MESH
 CENTRE_RE = 1.0 - 4.0 * PROP_RE
 CENTRE_IM = -4.0 * PROP_IM
@@ -183,8 +184,8 @@
 def window_kernel(
     sections, tiles,
     probe_ref, offsets_ref, phase_ref, absorption_ref, measured_ref, out_ref,
-    chain, field, probes, frames, waves, adjoint, partial, returned, shifts,
-    chain_send, chain_recv, plane_send, block_recv, corner_send, corner_recv,
+    own, field, probes, frames, waves, adjoint, partial, returned, shifts,
+    group_send, ready, plane_send, block_recv, corner_send, corner_recv,
     tile_send, tile_recv, aux_send, aux_recv, back_send, back_recv, shift_sem,
 ):
     slice_count, row_count, col_count = phase_ref.shape
@@ -241,29 +242,26 @@
         for part, value in enumerate(
             (CENTRE_RE * real - CENTRE_IM * imag, CENTRE_RE * imag + CENTRE_IM * real)
         ):
-            chain[group, layer, part, :, :col_count] = value
-            chain[group, layer, part, :, col_count:] = value[:, :LANES]
+            own[layer, part, :, :col_count] = value
+            own[layer, part, :, col_count:] = value[:, :LANES]
+    start = pl.multiple_of(group * LANES, LANES)
+    field[me, tile] = own[:, :, :, pl.ds(start, width)]
     probes[tile] = probe_ref[...]
     frames[tile] = measured_ref[pl.ds(tile * share, share)]
     ends = lax.div(group + groups - 1, groups) + lax.div(2 * groups - 2 - group, groups)
     pl.semaphore_wait(pltpu.get_barrier_semaphore(), tiles - 1 + len(across) + ends)
 
-    def span(at, direction):
-        return pl.ds((at + 1) * LANES, (groups - at) * LANES) if direction > 0 else pl.ds(0, (at + 1) * LANES)
-
-    def hop(source, at, direction):
-        part = chain.at[source, :, :, :, span(at, direction)]
+    def group_copy(at, target):
         return remote(
-            part, part, chain_send.at[source, (direction + 1) // 2], chain_recv.at[source],
-            me + direction * plane, tile,
-        )
-
-    def hops(at):
-        for source in range(groups):
-            if source <= at < groups - 1:
-                yield hop(source, at, 1)
-            if source >= at > 0:
-                yield hop(source, at, -1)
+            own.at[:, :, :, pl.ds(target * LANES, width)], field.at[me, tile], group_send.at[target],
+            block_recv.at[me], me + (target - at) * plane, tile,
+        )
+
+    def tell(direction, distance):
+        pl.semaphore_signal(
+            ready.at[(direction + 1) // 2, distance], inc=1,
+            device_id=device(me - direction * plane, tile), device_id_type=MESH,
+        )
 
     def plane_copy(source, view, axis):
         block = source * plane + place
@@ -277,6 +275,13 @@
         return remote(
             part, part, corner_send.at[source, axis], corner_recv.at[source, axis],
             group * plane + across[1 - axis], tile,
+        )
+
+    def far_copy(source):
+        view = field.at[source * plane + place, tile]
+        return remote(
+            view, view, corner_send.at[source, 0], corner_recv.at[source, 0],
+            group * plane + corner, tile,
         )
 
     def tile_copies(block, view):
@@ -314,48 +319,63 @@
                     value = jnp.where(chosen, pltpu.roll(value, 1 << bit, 1), value)
                 waves[0, index, part] = value[:, :width]
 
+    def ordered(at):
+        return sorted(range(groups), key=lambda source: (abs(source - at), source))
+
     def gather(at):
-        window = pl.ds(at * LANES, width)
-        order = sorted(range(groups), key=lambda source: (abs(source - at), source))
+        order = ordered(at)
+
+        def reach(distance):
+            for direction in (1, -1):
+                target = at + direction * distance
+                if 0 <= target < groups:
+                    if distance > 1:
+                        pl.semaphore_wait(ready.at[(direction + 1) // 2, distance], 1)
+                    group_copy(at, target).start()
+                    if 0 <= at - direction < groups:
+                        tell(direction, distance + 1)
 
         def spread_out(source):
-            if source <= at < groups - 1:
-                hop(source, at, 1).start()
-            if source >= at > 0:
-                hop(source, at, -1).start()
-            view = chain.at[source, :, :, :, window]
+            view = field.at[source * plane + place, tile]
             for axis in range(2):
                 plane_copy(source, view, axis).start()
+            if source in order[groups - DIRECT:]:
+                far_copy(source).start()
             for copy in tile_copies(source * plane + place, view):
                 copy.start()
-            field[source * plane + place, tile] = chain[source, :, :, :, window]
 
         def collect(source):
             for axis in range(2):
                 block = source * plane + across[axis]
                 arrived(field.at[block, tile], block_recv.at[block])
-                corner_copy(source, axis).start()
+                if source not in order[groups - DIRECT:]:
+                    corner_copy(source, axis).start()
                 for copy in tile_copies(block, field.at[block, tile]):
                     copy.start()
 
         def collect_corner(source):
             block = source * plane + corner
-            for axis in range(2):
-                arrived(field.at[block, tile, :, axis], corner_recv.at[source, axis])
+            if source in order[groups - DIRECT:]:
+                arrived(field.at[block, tile], corner_recv.at[source, 0])
+            else:
+                for axis in range(2):
+                    arrived(field.at[block, tile, :, axis], corner_recv.at[source, axis])
             for copy in tile_copies(block, field.at[block, tile]):
                 copy.start()
 
+        reach(1)
         for count in range(groups + 2):
             if count < groups:
                 source = order[count]
-                if source < at:
-                    arrived(chain.at[source, :, :, :, span(at - 1, 1)], chain_recv.at[source])
-                if source > at:
-                    arrived(chain.at[source, :, :, :, span(at + 1, -1)], chain_recv.at[source])
+                if source != at:
+                    block = source * plane + place
+                    arrived(field.at[block, tile], block_recv.at[block])
                 spread_out(source)
             if count == 0:
                 for copy in aux_copies():
                     copy.start()
+                for distance in range(2, groups):
+                    reach(distance)
             if 0 <= count - 1 < groups:
                 collect(order[count - 1])
             if 0 <= count - 2 < groups:
@@ -368,13 +388,32 @@
         def _():
             gather(at)
 
-    rows = lax.broadcasted_iota(jnp.int32, (height, width), 0)
-    first, last = rows == 0, rows == height - 1
+    rows = lax.broadcasted_iota(jnp.int32, (SUBLANES, width), 0)
+    lanes = lax.broadcasted_iota(jnp.int32, (height, LANES), 1)
+    first_row, last_row = rows == 0, rows == SUBLANES - 1
+    first_lane, last_lane = lanes == 0, lanes == LANES - 1
 
     def neighbours(value):
-        above = jnp.where(first, 0.0, pltpu.roll(value, 1, 0))
-        below = jnp.where(last, 0.0, pltpu.roll(value, height - 1, 0))
-        return (above + below) + (pltpu.roll(value, 1, 1) + pltpu.roll(value, width - 1, 1))
+        blocks = [value[at : at + SUBLANES] for at in range(0, height, SUBLANES)]
+        down = [0.0] + [pltpu.roll(block, 1, 0) for block in blocks]
+        up = [pltpu.roll(block, SUBLANES - 1, 0) for block in blocks] + [0.0]
+        vertical = jnp.concatenate(
+            [
+                jnp.where(first_row, down[at], down[at + 1]) + jnp.where(last_row, up[at + 1], up[at])
+                for at in range(len(blocks))
+            ],
+            0,
+        )
+        right = [pltpu.roll(value[:, at : at + LANES], 1, 1) for at in (0, LANES)]
+        left = [pltpu.roll(value[:, at : at + LANES], LANES - 1, 1) for at in (0, LANES)]
+        horizontal = jnp.concatenate(
+            [
+                right[0] + jnp.where(last_lane, left[1], left[0]),
+                jnp.where(first_lane, right[0], right[1]) + left[1],
+            ],
+            1,
+        )
+        return vertical + horizontal
 
     def spread(real, imag, ratio):
         real_sum, imag_sum = neighbours(real), neighbours(imag)
@@ -407,7 +446,6 @@
 
     lax.fori_loop(0, sections, forward, 0)
 
-    start = pl.multiple_of(group * LANES, LANES)
     following = pl.multiple_of(group_at(1) * LANES, LANES)
     for index in range(share):
         frame = jnp.concatenate(
@@ -493,12 +531,18 @@
     for at in range(groups):
         @pl.when(group == at)
         def _():
-            for copy in hops(at):
-                copy.wait_send()
+            for target in range(groups):
+                if target != at:
+                    group_copy(at, target).wait_send()
+            for count, source in enumerate(ordered(at)):
+                if count >= groups - DIRECT:
+                    far_copy(source).wait_send()
+                else:
+                    for axis in range(2):
+                        corner_copy(source, axis).wait_send()
     for source in range(groups):
         for axis in range(2):
             plane_copy(source, field.at[source * plane + place, tile], axis).wait_send()
-            corner_copy(source, axis).wait_send()
     for block in range(sections):
         for copy in tile_copies(block, field.at[block, tile]):
             copy.wait_send()
@@ -520,7 +564,7 @@
         in_specs=[vmem, pl.BlockSpec(memory_space=pl.ANY), vmem, vmem, vmem],
         out_specs=vmem,
         scratch_shapes=[
-            pltpu.VMEM((groups, slice_count, 2, row_count, col_count + LANES), jnp.float32),
+            pltpu.VMEM((slice_count, 2, row_count, col_count + LANES), jnp.float32),
             pltpu.VMEM((sections, tiles, slice_count, 2, row_count, width), jnp.float32),
             pltpu.VMEM((tiles, 2, row_count, col_count), jnp.float32),
             pltpu.VMEM((tiles, share, row_count, col_count), jnp.float32),
@@ -529,8 +573,8 @@
             pltpu.VMEM((groups, tiles, slice_count, 2, row_count, LANES), jnp.float32),
             pltpu.VMEM((groups, tiles, slice_count, 2, row_count, LANES), jnp.float32),
             pltpu.SMEM((probe_count,), jnp.int32),
-            dma((groups, 2)),
             dma((groups,)),
+            pltpu.SemaphoreType.REGULAR((2, groups)),
             dma((groups, 2)),
             dma((sections,)),
             dma((groups, 2)),

time: 35.4 us -> 31.5 us (0.89)
  Pallas kernels: 33.7 us -> 29.8 us
    pallas_call x1, Pallas kernels: 33.7 us -> 29.8 us  [windowed_body(): pl.pallas_call(functools.partial(window_kernel, sections, tiles), out_sha...]
where the time goes in v3:
time: 31.5 us; the launch traced here: 31.3 us
  Pallas kernels  29.8 us (95%)
  local copies, waits for them, and re-layouts  1.47 us (5%)
    pallas_call x1, Pallas kernels, windowed_body(): pl.pallas_call(functools.partial(window_kernel, sections, tiles), out_sha...  29.8 us
    unnamed x1, local copies, waits for them, and re-layouts  1.47 us

profile of v3, /device:TPU:0, one launch (start us, length us, event | category | flops | bytes accessed | tf_op | source)
XLA Modules:
  0.0 31.3 jit_solution(11690380526251241455)
XLA Ops:
  0.0 29.8 %shard_map.55 = f32[2,2,8,512]{3,2,1,0:T(8,128)} custom-call(f32[2,8,512]{2,1,0:T(8,128)} %probe_ref.1, s32[4]{0:T(128)} %offsets_ref.1, f32[2,8,512]{2,1,0:T(8,128)} %phase_ref.1, f32[2,8,512]{2,1,0:T(8,128)} %absorption_ref.1, f32[4,8,512]{2,1,0:T(8,128)} %measured_ref.1), custom_call_target="tpu_custom_call" | custom-call | tf_op jit(solution)/shard_map/pallas_call | solution.py:561
  29.8 1.5 %copy.7 = f32[2,2,8,512]{3,2,1,0:T(8,128)} copy(f32[2,2,8,512]{3,2,1,0:T(8,128)} %shard_map.55) | data formatting | bytes 131072
